TPU v7x, 256 devices: a whole 4x4x8 slice. The times are simulated.
256 devices in a mesh: req: 32 (over z_lo, y, x), tp: 8 (over z_hi, core).
Axes of the slice: x: 4, y: 4, z: 8 (z_hi: 4, z_lo: 2; z = z_hi * 2 + z_lo), core: 2. Of those that a mesh axis runs over, the one named last changes fastest.
Arguments:
- queries: bfloat16 [8192, 1024], P('req', 'tp'), may hold values from -8 to 8
- suffix_kv: bfloat16 [8192, 512], P('req'), may hold values from -6 to 6
- ssm_x: bfloat16 [8192, 3072], P('req', 'tp'), may hold values from -6 to 6
- ssm_z: bfloat16 [8192, 3072], P('req', 'tp'), may hold values from -6 to 6
- ssm_bc: bfloat16 [8192, 512], P('req'), may hold values from -1.5 to 1.5
- ssm_dt: float32 [8192, 24], P('req', 'tp'), may hold values from 0 to 1, as said below
- a_log: float32 [24], P('tp'), may hold values from -0.5 to 0.5
- d_skip: float32 [24], P('tp'), may hold values from 0.5 to 1.5
- prefix_kv: bfloat16 [32, 4096, 512], P('req'), may hold values from -10 to 10
- prefix_end_states: bfloat16 [32, 24, 128, 256], P('req', 'tp'), may hold values from -1.5 to 1.5
- w_attn_out: bfloat16 [1024, 3072], P('tp'), may hold values from -0.1875 to 0.1875
- w_ssm_out: bfloat16 [3072, 3072], P('tp'), may hold values from -0.109375 to 0.109375
- suffix_len: int32 [32], P('req'), may hold values from 32 to 256, as said below
- prefix_of: int32 [32], P('req'), may hold values from 0 to 3
- prefix_owner: int32 [4], replicated, may hold values from 0 to 31, as said below
Outputs:
- mixed: bfloat16 [8192, 3072], P(('req', 'tp'))
- end_state: float32 [32, 24, 128, 256], P('req', 'tp')
Inputs may be any that keep to these rules, and one draw needn't show every extreme that they name: `suffix_len`: some request has the full 256 tokens. `prefix_owner`: distinct slots. `ssm_dt`: positive.
All inputs are finite; a program needn't handle non-finite values.
Results may differ from a plain program's by a relative error of at most 0.014.
Values may be sent and summed in bfloat16 or wider, within the bound.
No kernel may reach another device: no remote copies, remote signals or barrier semaphores. Data moves between devices by JAX's collectives and lax.ppermute only.
A program may use at most 128 MiB of HBM per device.

v0:
```python
import jax
import jax.numpy as jnp
from jax import lax
from jax.sharding import PartitionSpec as P

HEAD_SIZE = 128
QH = 8
KEY_VALUE_HEADS = 2
CH = 256


def spread(shard, axis, root):
    mine = lax.axis_index(axis) == root
    return lax.psum(jnp.where(mine, shard, jnp.zeros_like(shard)), axis)


def absorb(running, query_rows, key_rows, value_rows, allowed):
    row_max, row_sum, weighted = running
    scores = jnp.einsum(
        "qhd,kd->hqk", query_rows, key_rows, preferred_element_type=jnp.float32
    ) * key_rows.shape[-1] ** (-0.5)
    if allowed is not None:
        scores = jnp.where(allowed[None], scores, -jnp.inf)
    new_max = jnp.maximum(row_max, jnp.max(scores, axis=-1))
    weights = jnp.exp(scores - new_max[..., None])
    factor = jnp.exp(row_max - new_max)
    row_sum = row_sum * factor + jnp.sum(weights, axis=-1)
    weighted = weighted * factor[..., None] + jnp.einsum(
        "hqk,kd->hqd", weights.astype(jnp.bfloat16), value_rows, preferred_element_type=jnp.float32
    )
    return (new_max, row_sum, weighted)


def advance(ssm_state, x_rows, b_rows, c_rows, dt_rows, decay_rate):
    span = x_rows.shape[0]
    position = jnp.arange(span)
    causal = position[:, None] >= position[None, :]
    cumulative = jnp.cumsum(dt_rows * decay_rate[None, :], axis=0)
    products = jnp.dot(c_rows, b_rows.T, preferred_element_type=jnp.float32)
    spread_log = cumulative.T[:, :, None] - cumulative.T[:, None, :]
    decays = jnp.exp(jnp.where(causal[None], spread_log, -jnp.inf))
    mixing = (decays * products[None] * dt_rows.T[:, None, :]).astype(jnp.bfloat16)
    outputs = jnp.einsum("hts,shp->thp", mixing, x_rows, preferred_element_type=jnp.float32)
    carried = jnp.einsum(
        "hpn,tn->thp", ssm_state.astype(jnp.bfloat16), c_rows, preferred_element_type=jnp.float32
    )
    outputs = outputs + jnp.exp(cumulative)[:, :, None] * carried
    remaining = jnp.exp(cumulative[-1][None, :] - cumulative) * dt_rows
    weighted = (x_rows.astype(jnp.float32) * remaining[:, :, None]).astype(jnp.bfloat16)
    ssm_state = jnp.exp(cumulative[-1])[:, None, None] * ssm_state + jnp.einsum(
        "shp,sn->hpn", weighted, b_rows, preferred_element_type=jnp.float32
    )
    return (ssm_state, outputs)


def mamba_part(ssm_x, ssm_z, ssm_bc, ssm_dt, a_log, d_skip, start_state, length, block_rows):
    row_count, full_width = ssm_x.shape
    head_count = ssm_dt.shape[1]
    head_dim = full_width // head_count
    state_dim = ssm_bc.shape[1] // 2
    block_rows = min(block_rows, row_count)
    blocks = row_count // block_rows
    live_rows = jnp.arange(row_count) < length
    dt_live = jnp.where(live_rows[:, None], ssm_dt, jnp.zeros_like(ssm_dt))
    decay_rate = -jnp.exp(a_log)
    x_parts = ssm_x.reshape(blocks, block_rows, head_count, head_dim)
    b_parts = ssm_bc[:, :state_dim].reshape(blocks, block_rows, state_dim)
    c_parts = ssm_bc[:, state_dim:].reshape(blocks, block_rows, state_dim)
    dt_parts = dt_live.reshape(blocks, block_rows, head_count)

    def fold_block(ssm_state, pieces):
        return advance(ssm_state, pieces[0], pieces[1], pieces[2], pieces[3], decay_rate)

    end_state, outputs = lax.scan(fold_block, start_state, (x_parts, b_parts, c_parts, dt_parts))
    skipped = d_skip[None, :, None] * ssm_x.reshape(row_count, head_count, head_dim).astype(
        jnp.float32
    )
    outputs = outputs.reshape(row_count, head_count, head_dim) + skipped
    gated = outputs.reshape(row_count, full_width) * jax.nn.silu(ssm_z.astype(jnp.float32))
    gated = jnp.where(live_rows[:, None], gated, jnp.zeros_like(gated)).astype(jnp.bfloat16)
    return (gated, end_state)


def body(
    queries,
    suffix_kv,
    ssm_x,
    ssm_z,
    ssm_bc,
    ssm_dt,
    a_log,
    d_skip,
    prefix_kv,
    prefix_end_states,
    w_attn_out,
    w_ssm_out,
    suffix_len,
    prefix_of,
    prefix_owner,
):
    tp_index = lax.axis_index("tp")
    row_count = queries.shape[0]
    head_count = queries.shape[1] // HEAD_SIZE
    length = suffix_len[0]
    wanted = prefix_of[0]
    kv_head = tp_index * head_count // (QH // KEY_VALUE_HEADS)
    query_rows = queries.reshape(row_count, head_count, HEAD_SIZE)
    running = (
        jnp.full((head_count, row_count), -jnp.inf, jnp.float32),
        jnp.zeros((head_count, row_count), jnp.float32),
        jnp.zeros((head_count, row_count, HEAD_SIZE), jnp.float32),
    )
    chosen_state = jnp.zeros_like(prefix_end_states[0])
    own_head = lax.dynamic_slice_in_dim(prefix_kv[0], kv_head * 2 * HEAD_SIZE, 2 * HEAD_SIZE, 1)
    chosen_kv = jnp.zeros_like(own_head)
    for prefix in range(prefix_owner.shape[0]):
        got_kv, got_state = (
            spread(own_head, "req", prefix_owner[prefix]),
            spread(prefix_end_states[0], "req", prefix_owner[prefix]),
        )
        chosen_kv = jnp.where(wanted == prefix, got_kv, chosen_kv)
        chosen_state = jnp.where(wanted == prefix, got_state, chosen_state)
    key_count = chosen_kv.shape[0]
    block_keys = min(1024, key_count)
    key_blocks = chosen_kv.reshape(key_count // block_keys, block_keys, 2 * HEAD_SIZE)

    def absorb_block(carried, piece):
        return (absorb(carried, query_rows, piece[:, :HEAD_SIZE], piece[:, HEAD_SIZE:], None), None)

    running, unused = lax.scan(absorb_block, running, key_blocks)
    fresh = lax.dynamic_slice_in_dim(suffix_kv, kv_head * 2 * HEAD_SIZE, 2 * HEAD_SIZE, 1)
    position = jnp.arange(row_count)
    causal = position[None, :] <= position[:, None]
    running = absorb(running, query_rows, fresh[:, :HEAD_SIZE], fresh[:, HEAD_SIZE:], causal)
    row_max, row_sum, weighted = running
    live_rows = position < length
    attention = (
        (weighted / row_sum[..., None])
        .transpose(1, 0, 2)
        .reshape(row_count, head_count * HEAD_SIZE)
    )
    attention = jnp.where(live_rows[:, None], attention, jnp.zeros_like(attention)).astype(
        jnp.bfloat16
    )
    gated, end_state = mamba_part(
        ssm_x, ssm_z, ssm_bc, ssm_dt, a_log, d_skip, chosen_state.astype(jnp.float32), length, CH
    )
    mixed = lax.psum_scatter(
        (
            jnp.dot(attention, w_attn_out, preferred_element_type=jnp.float32)
            + jnp.dot(gated, w_ssm_out, preferred_element_type=jnp.float32)
        ).astype(jnp.bfloat16),
        "tp",
        scatter_dimension=0,
        tiled=True,
    )
    return (mixed, end_state[None])


def solution(mesh):
    in_specs = (
        P("req", "tp"),
        P("req", None),
        P("req", "tp"),
        P("req", "tp"),
        P("req", None),
        P("req", "tp"),
        P("tp"),
        P("tp"),
        P("req", None, None),
        P("req", "tp", None, None),
        P("tp", None),
        P("tp", None),
        P("req"),
        P("req"),
        P(),
    )
    out_specs = (P(("req", "tp"), None), P("req", "tp", None, None))
    return jax.shard_map(body, mesh=mesh, in_specs=in_specs, out_specs=out_specs, check_vma=False)
```

profile of v0, /device:TPU:32, one launch (start us, length us, event | category | flops | bytes accessed | tf_op | source)
XLA Modules:
  0.0 458.7 jit_solution(11247897547385871600)
XLA Ops:
  7.2 1.5 fusion.75
  11.4 1.8 select_bitcast_fusion.4
  13.2 6.0 %select_bitcast_fusion = (bf16[4096,256]{1,0:T(8,128)(2,1)}, bf16[4096,256]{1,0:T(8,128)(2,1)}, bf16[4096,256]{1,0:T(8,128)(2,1)}, bf16[4096,256]{1,0:T(8,128)(2,1)}) fusion(pred[]{:T(512)S(6)} %eq.55, bf16[1,4096,512]{2,1,0:T(8,128)(2,1)} %param.25, s32[]{:T(128)S(6)} %select_n.157, pred[]{:T(512)S(6)} %eq.49, pred[]{:T(512)S(6)} %eq.52, pred[]{:T(512)S(6)} %eq.46), kind=kLoop, calls=%fused_computation.23 | loop fusion | flops 4194304 | bytes 10485768 | tf_op jit(solution)/shard_map/jit(_where)/select_n | solution.py:14
  20.9 0.9 reduce-window.6
  23.3 2.3 fusion.76
  25.7 0.9 fusion.54
  26.6 347.4 %all-reduce.3.cloned.1.call-done = (bf16[4096,256]{1,0:T(8,128)(2,1)}, bf16[4096,256]{1,0:T(8,128)(2,1)}, bf16[4096,256]{1,0:T(8,128)(2,1)}, bf16[4096,256]{1,0:...) async-done(((bf16[4096,256]{1,0:T(8,128)(2,1)}, ...) | async-done | bytes 9175056 | tf_op jit(solution)/shard_map/psum | solution.py:14
  374.0 1.0 select_select_fusion.1
  375.9 1.4 fusion.16
  377.3 0.9 copy.25
  378.2 3.3 select_select_fusion
  381.5 18.7 %while.4 = (s32[]{:T(128)}, f32[1,256]{1,0:T(1,128)S(1)}, f32[1,256]{1,0:T(1,128)S(1)}, f32[1,256,128]{2,1,0:T(8,128)S(1)}, bf16[4,1024,256]{2,1,0:T(8,128)(2,1)...) while((s32[]{:T(128)}, f32[1,256]{1,0:T(1,128)S(1)}, f32[1,256]{1,0:T(1,128)S(1)}, ...), condition=%wide.region_7.8_spmd.clone, body=%wide.region_4.7_spmd.clone.sunk | while | flops 135890176 | bytes 7159937 | solution.py:130
  381.5 1.1 dynamic-slice_bitcast_fusion.2
  382.6 0.8 copy-done.1
  383.4 1.2 fusion.91
  384.9 1.3 fusion.95
  386.2 1.1 dynamic-slice_bitcast_fusion.2
  387.3 0.8 copy-done.1
  388.1 1.2 fusion.91
  389.5 1.3 fusion.95
  390.9 1.1 dynamic-slice_bitcast_fusion.2
  392.8 1.2 fusion.91
  394.2 1.3 fusion.95
  395.6 1.1 dynamic-slice_bitcast_fusion.2
  396.6 0.8 copy-done.1
  397.4 1.2 fusion.91
  398.9 1.3 fusion.95
  400.9 1.0 fusion.37
  402.0 3.7 fusion.24
  405.7 4.4 fusion.13
  410.1 1.0 fusion.14
  411.1 40.7 %reduce-scatter.2.cloned.1.call-done = bf16[32,3072]{1,0:T(8,128)(2,1)} async-done(((bf16[256,3072]{1,0:T(8,128)(2,1)}), bf16[32,3072]{1,0:T(8,128)(2,1)}) %reduce-scatter.2.cloned.1.call-update) | async-done | bytes 196624 | tf_op jit(solution)/shard_map/reduce_scatter | solution.py:148
  (82 shorter events, 5.2 us)
Async XLA Ops:
  7.2 398.5 %copy-start = (bf16[384,3072]{1,0:T(8,128)(2,1)S(1)}, bf16[384,3072]{1,0:T(8,128)(2,1)}, u32[]{:S(2)}) copy-start(bf16[384,3072]{1,0:T(8,128)(2,1)} %param.28) | copy-start | bytes 7077892
  7.2 366.8 %all-reduce.3.cloned.1.call-start = ((), (), s32[]{:S(2)}) async-start(), calls=%async_computation.2 | async-start | bytes 18350080 | tf_op jit(solution)/shard_map/psum | solution.py:14
  19.2 1.5 copy-start.17
  19.2 1.6 copy-start.10
  19.2 3.0 copy-start.9
  19.2 3.4 copy-start.16
  19.3 6.4 %copy-start.5 = (bf16[256,512]{1,0:T(8,128)(2,1)S(1)}, bf16[256,512]{1,0:T(8,128)(2,1)}, u32[]{:S(2)}) copy-start(bf16[256,512]{1,0:T(8,128)(2,1)} %param.21) | copy-start | bytes 786436
  19.3 432.5 %reduce-scatter.2.cloned.1.call-start = ((), (), s32[]{:S(2)}) async-start(), calls=%async_computation.1 | async-start | bytes 1769472 | tf_op jit(solution)/shard_map/reduce_scatter | solution.py:148
  20.8 356.5 %copy-start.11 = (pred[256]{0:T(512)(128)(4,1)}, pred[256]{0:T(512)(128)(4,1)S(1)}, u32[]{:S(2)}) copy-start(pred[256]{0:T(512)(128)(4,1)S(1)} %iota_compare_fusion.2) | copy-start | bytes 772
  22.4 354.9 %copy-start.7 = (bf16[256,384]{0,1:T(8,128)(2,1)}, bf16[256,384]{0,1:T(8,128)(2,1)S(1)}, u32[]{:S(2)}) copy-start(bf16[256,384]{0,1:T(8,128)(2,1)S(1)} %copy.24) | copy-start | bytes 589828
  22.6 354.7 %copy-start.14 = (f32[3]{0:T(128)}, f32[3]{0:T(128)S(1)}, u32[]{:S(2)}) copy-start(f32[3]{0:T(128)S(1)} %slice_reduce_fusion) | copy-start | bytes 40
  375.0 0.7 copy-start.2
  382.6 0.8 copy-start.1
  387.3 0.8 copy-start.1
  392.0 0.8 copy-start.1
  396.6 0.8 copy-start.1
  401.9 3.7 copy-start.4
  401.9 3.7 copy-start.12
  401.9 3.7 copy-start.13
  405.7 4.4 copy-start.15
  405.7 4.4 copy-start.3
  405.7 4.4 copy-start.6
  405.7 4.4 copy-start.8
Sparse Core Ops, SparseCore 0:
  19.4 354.5 all-reduce.2
  410.2 41.5 reduce-scatter.1
where the time goes:
time: 461 us; the launch traced here: 459 us
  waiting for transfers between devices  388 us (84%)
  matrix products  23.9 us (5%)
  between operations  18.4 us (4%)
  other arithmetic  16 us (3%)
  local copies, waits for them, and re-layouts  12 us (3%)
    psum x1, waiting for transfers between devices, spread(): return lax.psum(jnp.where(mine, shard, jnp.zeros_like(shard)), axis)  347 us
    reduce_scatter x1, waiting for transfers between devices, body(): lax.psum_scatter((jnp.dot(attention, w_attn_out, preferred_element_type=j...  40.7 us
  transfers between devices with their start and end apart: 2, of which 2 were waited for; matrix products, arithmetic and copies ran while one was open for 1% of the time, Pallas kernels for 0%

commit v1 on v0

v1 whole, which is shorter than its diff:
```python
import jax
import jax.numpy as jnp
from jax import lax
from jax.experimental import pallas as pl
from jax.sharding import PartitionSpec as P

HEAD = 128
QH = 8
KVH = 2
REQ = 32
TP = 8
GROUP = 4
TAG_ROWS = 4
F32 = jnp.float32
BF16 = jnp.bfloat16


def exchange(value, axis, count, step):
    return lax.ppermute(value, axis, [(i, step(i)) for i in range(count)])


def split3(value):
    high = value.astype(BF16)
    rest = value - high.astype(F32)
    mid = rest.astype(BF16)
    low = (rest - mid.astype(F32)).astype(BF16)
    return high, mid, low


def spread_slots(prefix_kv, states, quarter, kv_head, prefix):
    rows = prefix_kv.shape[1] // GROUP
    piece = lax.dynamic_slice(
        prefix_kv[0], (quarter * rows, kv_head * 2 * HEAD), (rows, 2 * HEAD)
    )
    pieces = states[0].reshape(REQ, -1, 2 * HEAD)
    tag = jnp.broadcast_to(prefix.astype(BF16), (REQ, TAG_ROWS, 2 * HEAD))
    return jnp.concatenate([piece.reshape(REQ, -1, 2 * HEAD), pieces, tag], 1)


def pick_slots(chunks, prefix_owner):
    wanted = chunks[:, -1:, :].astype(F32)
    choice = lax.dynamic_index_in_dim(chunks, prefix_owner[0], 0)
    picked = jnp.broadcast_to(choice, chunks.shape)
    for prefix in range(1, prefix_owner.shape[0]):
        choice = lax.dynamic_index_in_dim(chunks, prefix_owner[prefix], 0)
        picked = jnp.where(wanted == prefix, choice, picked)
    return picked


def dot(left, right, contract):
    return lax.dot_general(left, right, (contract, ((), ())), preferred_element_type=F32)


def attention_kernel(q0, q1, q2, q3, cached, fresh, own_ref, log_ref, message_ref):
    keys = cached[:, :HEAD]
    values = cached[:, HEAD:]
    scale = HEAD ** (-0.5)
    for h, query in enumerate((q0, q1, q2, q3)):
        scores = dot(keys, query[...], ((1,), (1,))) * scale
        top = jnp.max(scores, 0, keepdims=True)
        if h == 0:
            own = dot(fresh[:, :HEAD], query[...], ((1,), (1,))) * scale
            key_at = lax.broadcasted_iota(jnp.int32, own.shape, 0)
            query_at = lax.broadcasted_iota(jnp.int32, own.shape, 1)
            own = jnp.where(key_at <= query_at, own, -jnp.inf)
            top = jnp.maximum(top, jnp.max(own, 0, keepdims=True))
        weights = jnp.exp(scores - top)
        total = jnp.sum(weights, 0, keepdims=True)
        out = dot(values, weights.astype(BF16), ((0,), (0,)))
        if h == 0:
            own = jnp.exp(own - top)
            total = total + jnp.sum(own, 0, keepdims=True)
            out = out + dot(fresh[:, HEAD:], own.astype(BF16), ((0,), (0,)))
        logs = top + jnp.log(total)
        normal = out / total
        if h == 0:
            own_ref[...] = normal
            log_ref[...] = logs
        else:
            high, mid, low = (part.astype(F32) for part in split3(logs))
            row = lax.broadcasted_iota(jnp.int32, (16, logs.shape[1]), 0)
            stats = jnp.where(row == 0, high, jnp.where(row == 1, mid, jnp.where(row == 2, low, 0.0)))
            message_ref[h - 1, :HEAD, :] = normal.astype(BF16)
            message_ref[h - 1, HEAD:, :] = stats.astype(BF16)


def body(
    queries,
    suffix_kv,
    ssm_x,
    ssm_z,
    ssm_bc,
    ssm_dt,
    a_log,
    d_skip,
    prefix_kv,
    prefix_end_states,
    w_attn_out,
    w_ssm_out,
    suffix_len,
    prefix_of,
    prefix_owner,
):
    tp = lax.axis_index("tp")
    rows = queries.shape[0]
    length = suffix_len[0]
    kv_head = tp // GROUP
    quarter = tp % GROUP

    with jax.named_scope("spread"):
        sent = spread_slots(prefix_kv, prefix_end_states, quarter, kv_head, prefix_of[0])
        chunks = lax.all_to_all(sent, "req", 0, 0)
    with jax.named_scope("queries_exchange"):
        heads = [queries] + [exchange(queries, "tp", TP, lambda i, k=k: i ^ k) for k in (1, 2, 3)]
    with jax.named_scope("fetch"):
        got = lax.all_to_all(pick_slots(chunks, prefix_owner), "req", 0, 0)
    key_rows = prefix_kv.shape[1] // GROUP // REQ
    cached = got[:, :key_rows].reshape(-1, 2 * HEAD)
    state = got[:, key_rows:-TAG_ROWS].reshape(prefix_end_states.shape[1:])

    with jax.named_scope("attention"):
        fresh = lax.dynamic_slice_in_dim(suffix_kv, kv_head * 2 * HEAD, 2 * HEAD, 1)
        normal, logs, messages = pl.pallas_call(
            attention_kernel,
            out_shape=(
                jax.ShapeDtypeStruct((HEAD, rows), F32),
                jax.ShapeDtypeStruct((1, rows), F32),
                jax.ShapeDtypeStruct((GROUP - 1, HEAD + 16, rows), BF16),
            ),
            name="attention_kernel",
        )(*heads, cached, fresh)
        arrived = [exchange(messages[k - 1], "tp", TP, lambda i, k=k: i ^ k) for k in (1, 2, 3)]

    with jax.named_scope("mamba"):
        position = jnp.arange(rows)
        live = position < length
        head_count = ssm_dt.shape[1]
        dt = jnp.where(live[:, None], ssm_dt, 0.0)
        rate = -jnp.exp(a_log)
        b_rows = ssm_bc[:, : 2 * HEAD]
        c_rows = ssm_bc[:, 2 * HEAD :]
        x = ssm_x.reshape(rows, head_count, HEAD)
        log_decay = jnp.cumsum(dt * rate[None, :], axis=0)
        back = position[:, None] >= position[None, :]
        products = jnp.dot(c_rows, b_rows.T, preferred_element_type=F32)
        diff = log_decay.T[:, :, None] - log_decay.T[:, None, :]
        decays = jnp.exp(jnp.where(back[None], diff, -jnp.inf))
        mixing = (decays * products[None] * dt.T[:, None, :]).astype(BF16)
        y = jnp.einsum("hts,shp->thp", mixing, x, preferred_element_type=F32)
        y = y + d_skip[None, :, None] * x.astype(F32)
        remaining = jnp.exp(log_decay[-1][None, :] - log_decay) * dt
        weighted = (x.astype(F32) * remaining[:, :, None]).astype(BF16)
        fresh_state = jnp.einsum("shp,sn->hpn", weighted, b_rows, preferred_element_type=F32)
        carried = jnp.einsum("hpn,tn->thp", state, c_rows, preferred_element_type=F32)
        y = y + jnp.exp(log_decay)[:, :, None] * carried
        end_state = jnp.exp(log_decay[-1])[:, None, None] * state.astype(F32) + fresh_state
        gated = y.reshape(rows, -1) * jax.nn.silu(ssm_z.astype(F32))
        gated = jnp.where(live[:, None], gated, 0.0).astype(BF16)
        gated_out = jnp.dot(gated, w_ssm_out, preferred_element_type=F32)
        arrived, gated_out = lax.optimization_barrier((arrived, gated_out))

    with jax.named_scope("combine"):
        other_logs = [jnp.sum(m[HEAD : HEAD + 3].astype(F32), 0) for m in arrived]
        all_logs = [logs[0]] + other_logs
        top = jnp.maximum(jnp.maximum(all_logs[0], all_logs[1]), jnp.maximum(all_logs[2], all_logs[3]))
        scale = [jnp.exp(v - top) for v in all_logs]
        total = scale[0] + scale[1] + scale[2] + scale[3]
        mixed_t = normal * scale[0]
        for k in range(3):
            mixed_t = mixed_t + arrived[k][:HEAD].astype(F32) * scale[k + 1]
        attention = (mixed_t / total).T
        attention = jnp.where(live[:, None], attention, 0.0).astype(BF16)

    with jax.named_scope("project"):
        partial = (
            jnp.dot(attention, w_attn_out, preferred_element_type=F32) + gated_out
        ).astype(BF16)
    with jax.named_scope("reduce"):
        mixed = reduce_rows(partial, tp)
    return mixed, end_state[None]


def reduce_rows(partial, tp):
    width = partial.shape[1]
    place = tp // 2
    core = tp % 2
    blocks = partial.reshape(4, 2, -1, width)
    keep = lax.dynamic_index_in_dim(blocks, core, 1, keepdims=False)
    give = lax.dynamic_index_in_dim(blocks, 1 - core, 1, keepdims=False)
    come = exchange(give, "tp", TP, lambda i: i ^ 1)
    chip = (keep.astype(F32) + come.astype(F32)).astype(BF16)
    half = chip.shape[1] // 2

    def part(offset, first):
        block = lax.dynamic_index_in_dim(chip, (place + offset) % 4, 0, keepdims=False)
        return block[:half] if first else block[half:]

    up = lambda value: exchange(value, "tp", TP, lambda i: (i + 2) % TP)
    down = lambda value: exchange(value, "tp", TP, lambda i: (i - 2) % TP)
    from_below = up(jnp.stack([part(2, True), part(1, False)]))
    from_above = down(jnp.stack([part(2, False), part(3, True)]))
    via_up = up((part(1, True).astype(F32) + from_below[0].astype(F32)).astype(BF16))
    via_down = down((part(3, False).astype(F32) + from_above[0].astype(F32)).astype(BF16))
    first = part(0, True).astype(F32) + via_up.astype(F32) + from_above[1].astype(F32)
    last = part(0, False).astype(F32) + via_down.astype(F32) + from_below[1].astype(F32)
    return jnp.concatenate([first, last], 0).astype(BF16)


def solution(mesh):
    in_specs = (
        P("req", "tp"),
        P("req", None),
        P("req", "tp"),
        P("req", "tp"),
        P("req", None),
        P("req", "tp"),
        P("tp"),
        P("tp"),
        P("req", None, None),
        P("req", "tp", None, None),
        P("tp", None),
        P("tp", None),
        P("req"),
        P("req"),
        P(),
    )
    out_specs = (P(("req", "tp"), None), P("req", "tp", None, None))
    return jax.shard_map(body, mesh=mesh, in_specs=in_specs, out_specs=out_specs, check_vma=False)
```

time: 461 us -> 108 us (0.23)
  waiting for transfers between devices: 388 us -> 27.8 us
  starting transfers between devices: 0.08 us -> 33.3 us
  matrix products: 23.9 us -> 8.86 us
  between operations: 18.4 us -> 10.2 us
  other arithmetic: 16 us -> 9.29 us
  Pallas kernels: 0 us -> 4.84 us
    psum x1 -> x0, waiting for transfers between devices: 347 us -> none  [spread(): return lax.psum(jnp.where(mine, shard, jnp.zeros_like(shard)), axis)]
    reduce_scatter x1 -> x0, waiting for transfers between devices: 40.7 us -> none  [body(): lax.psum_scatter((jnp.dot(attention, w_attn_out, preferred_element_type=j...]
    ppermute x0 -> x11, waiting for transfers between devices: none -> 20 us  [exchange(): return lax.ppermute(value, axis, [(i, step(i)) for i in range(count)])]
    ppermute x0 -> x11, starting transfers between devices: none -> 16.9 us  [exchange(): return lax.ppermute(value, axis, [(i, step(i)) for i in range(count)])]
    all_to_all x0 -> x2, starting transfers between devices: none -> 16.4 us  [the longest x1 8.55 us: body(): chunks = lax.all_to_all(sent, 'req', 0, 0)]
    dot_general x15 -> x6, matrix products: 23.9 us -> 8.86 us  [the longest x1 2.07 us: body(): jnp.einsum('hpn,tn->thp', state, c_rows, preferred_element_type=F32)]
    select_n x4 -> x1, other arithmetic: 12.2 us -> 1.05 us  [pick_slots(): picked = jnp.where(wanted == prefix, choice, picked)]
    all_to_all x0 -> x2, waiting for transfers between devices: none -> 7.78 us  [the longest x1 7.2 us: body(): got = lax.all_to_all(pick_slots(chunks, prefix_owner), 'req', 0, 0)]
  transfers between devices with their start and end apart: 2 -> 13, of which waited for: 2 -> 8; matrix products, arithmetic and copies ran while one was open for 1% -> 18% of each run, Pallas kernels for 0% -> 0%
where the time goes in v1:
time: 108 us; the launch traced here: 107 us
  starting transfers between devices  33.3 us (31%)
  waiting for transfers between devices  27.8 us (26%)
  local copies, waits for them, and re-layouts  12.7 us (12%)
  between operations  10.2 us (9%)
  other arithmetic  9.29 us (9%)
  matrix products  8.86 us (8%)
  Pallas kernels  4.84 us (4%)
    ppermute x11, waiting for transfers between devices, exchange(): return lax.ppermute(value, axis, [(i, step(i)) for i in range(count)])  20 us
    ppermute x11, starting transfers between devices, exchange(): return lax.ppermute(value, axis, [(i, step(i)) for i in range(count)])  16.9 us
    all_to_all x1, starting transfers between devices, body(): chunks = lax.all_to_all(sent, 'req', 0, 0)  8.55 us
    all_to_all x1, starting transfers between devices, body(): got = lax.all_to_all(pick_slots(chunks, prefix_owner), 'req', 0, 0)  7.89 us
    all_to_all x1, waiting for transfers between devices, body(): got = lax.all_to_all(pick_slots(chunks, prefix_owner), 'req', 0, 0)  7.2 us
    pallas_call x1, Pallas kernels, body(): pl.pallas_call(attention_kernel, out_shape=(jax.ShapeDtypeStruct((HEAD, r...  4.84 us
    unnamed x28, local copies, waits for them, and re-layouts  2.31 us
  transfers between devices with their start and end apart: 13, of which 8 were waited for; matrix products, arithmetic and copies ran while one was open for 18% of the time, Pallas kernels for 0%

profile of v1, /device:TPU:32, one launch (start us, length us, event | category | flops | bytes accessed | tf_op | source)
XLA Modules:
  0.0 107.0 jit_solution(14637379638423192899)
XLA Ops:
  1.5 1.0 squeeze.52
  2.6 1.1 %constant_dynamic-slice_fusion.5 = bf16[1,1024,256]{2,1,0:T(8,128)(2,1)S(1)} fusion(bf16[1,4096,512]{2,1,0:T(8,128)(2,1)} %param.23, s32[]{:T(128)S(6)} %select_n.114, s32[]{:T(128)S(6)} %select_n.116), kind=kLoop, calls=%fused_computation.98 | loop fusion | bytes 1048584 | tf_op jit(solution)/shard_map/spread/dynamic_slice | solution.py:32
  3.7 1.2 %maximum_maximum_fusion = bf16[32,48,256]{2,1,0:T(8,128)(2,1)} fusion(bf16[32,12,256]{2,1,0:T(8,128)(2,1)S(1)} %squeeze.52, bf16[32,32,256]{2,1,0:T(8,128)(2,1)S(1)} %bitcast.122, bf16[48]{0:T(256)(128)(2,1)S(1)} %pad.8.clone), kind=kLoop, calls=%fused_computation.10 | loop fusion | flops 2359296 | bytes 1507424 | tf_op jit(solution)/shard_map/spread/concatenate | solution.py:37
  4.8 8.6 %all-to-all-start = ((bf16[32,48,256]{2,1,0:T(8,128)(2,1)}), bf16[32,48,256]{2,1,0:T(8,128)(2,1)S(1)}, u32[]{:S(2)}, u32[]{:S(2)}) async-start(bf16[32,48,256]{2,1,0:T(8,128)(2,1)} %maximum_maximum_fusion), calls=%async_computation | async-start | bytes 1572864 | tf_op jit(solution)/shard_map/spread/all_to_all | solution.py:112
  13.4 3.4 %collective-permute-start.1 = (bf16[256,128]{1,0:T(8,128)(2,1)}, bf16[256,128]{1,0:T(8,128)(2,1)}, u32[]{:S(2)}, u32[]{:S(2)}) collective-permute-start(bf16[256,128]{1,0:T(8,128)(2,1)} %q0.1), channel_id=1, source_target_pairs={{0,2},{1,3},{2,0},{3,1},{4,6},{5,7},{6,4},{7,5},{8,10},{9,11},{10,... | collective-permute-start | bytes 196616 | tf_op jit(solution)/shard_map/queries_exchange/ppermute | solution.py:19
  26.9 1.1 select_select_fusion
  27.9 7.9 %all-to-all-start.1 = ((bf16[32,48,256]{2,1,0:T(8,128)(2,1)}), bf16[32,48,256]{2,1,0:T(8,128)(2,1)S(1)}, u32[]{:S(2)}, u32[]{:S(2)}) async-start(bf16[32,48,256]{2,1,0:T(8,128)(2,1)} %select_select_fusion), calls=%async_computation.1 | async-start | bytes 1572864 | tf_op jit(solution)/shard_map/fetch/all_to_all | solution.py:116
  35.9 0.9 reduce-window.6
  37.3 1.1 copy.30
  38.6 1.6 %constant_dynamic-slice_fusion.4.fresh = bf16[256,256]{1,0:T(8,128)(2,1)} fusion(bf16[256,512]{1,0:T(8,128)(2,1)} %param.16, s32[]{:T(128)S(6)} %select_n.116), kind=kLoop, calls=%fused_computation.97 | loop fusion | bytes 262148 | tf_op jit(solution)/shard_map/attention/dynamic_slice | solution.py:122
  40.2 1.2 %fusion.30 = f32[256,256]{1,0:T(8,128)S(1)} fusion(bf16[256,512]{1,0:T(8,128)(2,1)} %param.19), kind=kOutput, calls=%fused_computation.52 | convolution fusion | flops 33554432 | bytes 524288 | tf_op jit(solution)/shard_map/mamba/dot_general | solution.py:145
  41.4 1.2 %fusion.3 = f32[256,3,128]{0,2,1:T(8,128)} fusion(bf16[256,3,128]{0,2,1:T(8,128)(2,1)S(1)} %bitcast.124, f32[3,256]{1,0:T(4,128)S(1)} %get-tuple-element.40, f32[256,256]{1,0:T(8,128)S(1)} %fusion.30, f32[3,256]{1,0:T(4,128)S(1)} %bitcast.128, pred[256,256]{1,0:T(8,128)(4,1)S(1)} %iota_compare_fusion, f32[3]{0:T(128)S(1)} %copy-done.11), kind=kOutput, calls=%fused_computation.8 | convolution fusion | flops 51609600 | bytes 923660 | tf_op jit(solution)/shard_map/mamba/hts,shp->thp/dot_general | solution.py:149
  42.6 7.2 %all-to-all-done.1 = bf16[32,48,256]{2,1,0:T(8,128)(2,1)S(1)} async-done(((bf16[32,48,256]{2,1,0:T(8,128)(2,1)}), bf16[32,48,256]{2,1,0:T(8,128)(2,1)S(1)}, u32[]{:S(2)}, u32[]{:S(2)}) %all-to-all-start.1) | async-done | bytes 786464 | tf_op jit(solution)/shard_map/fetch/all_to_all | solution.py:116
  50.5 1.0 reshape.142
  51.5 2.1 %fusion.4 = f32[256,3,128]{0,2,1:T(8,128)} fusion(f32[256,3,128]{0,2,1:T(8,128)} %fusion.3, bf16[3,128,256]{2,1,0:T(8,128)(2,1)S(1)} %reshape.142, f32[256,3]{0,1:T(4,128)S(1)} %get-tuple-element.41, bf16[256,512]{1,0:T(8,128)(2,1)} %param.19), kind=kOutput, calls=%fused_computation.9 | convolution fusion | flops 50528256 | bytes 1117184 | tf_op jit(solution)/shard_map/mamba/hpn,tn->thp/dot_general | solution.py:154
  53.6 1.9 %copy.31 = f32[256,384]{1,0:T(8,128)} copy(f32[256,384]{0,1:T(8,128)} %bitcast.123) | data formatting | bytes 786432 | tf_op jit(solution)/shard_map/mamba/reshape | solution.py:157
  56.4 4.8 %attention_kernel.1 = (f32[128,256]{1,0:T(8,128)}, f32[1,256]{1,0:T(1,128)}, bf16[3,144,256]{2,1,0:T(8,128)(2,1)}) custom-call(bf16[256,128]{1,0:T(8,128)(2,1)} %q0.1, bf16[256,128]{1,0:T(8,128)(2,1)} %collective-permute-done.q1, bf16[256,128]{1,0:T(8,128)(2,1)} %collective-permute-done.1.q2, bf16[256,128]{1,0:T(8,128)(2,1)} %collective-permute-done.2.q3, ...), custom_call_target="tpu_custom_call" | custom-call | tf_op jit(solution)/shard_map/attention/attention_kernel/pallas_call | solution.py:123
  61.2 1.0 slice_bitcast_fusion.2
  62.3 2.4 %collective-permute-start.4 = (bf16[144,256]{1,0:T(8,128)(2,1)S(1)}, bf16[144,256]{1,0:T(8,128)(2,1)S(1)}, u32[]{:S(2)}, u32[]{:S(2)}) collective-permute-start(bf16[144,256]{1,0:T(8,128)(2,1)S(1)} %get-tuple-element.37), channel_id=1, source_target_pairs={{0,2},{1,3},{2,0},{3,1},{4,6},{5,7},{6,4},{7,5},{8,10},{9,11},{10,... | collective-permute-start | bytes 221192 | tf_op jit(solution)/shard_map/attention/ppermute | solution.py:19
  65.0 2.0 %fusion.18 = f32[256,3072]{1,0:T(8,128)S(1)} fusion(bf16[384,3072]{1,0:T(8,128)(2,1)S(1)} %copy-done, f32[256,384]{1,0:T(8,128)S(1)} %copy-done.2, bf16[256,384]{1,0:T(8,128)(2,1)} %param.18, pred[256]{0:T(512)(128)(4,1)S(1)} %iota_compare_fusion.1), kind=kOutput, calls=%fused_computation.32 | convolution fusion | flops 604766208 | bytes 6095104 | tf_op jit(solution)/shard_map/mamba/dot_general | solution.py:159
  67.8 1.8 %collective-permute-done.4 = bf16[144,256]{1,0:T(8,128)(2,1)S(1)} collective-permute-done((bf16[144,256]{1,0:T(8,128)(2,1)S(1)}, bf16[144,256]{1,0:T(8,128)(2,1)S(1)}, u32[]{:S(2)}, u32[]{:S(2)}) %collective-permute-start.4) | collective-permute-done | bytes 73760 | tf_op jit(solution)/shard_map/attention/ppermute | solution.py:19
  70.4 1.2 %copy-done.1 = bf16[256,3072]{1,0:T(8,128)(2,1)} copy-done((bf16[256,3072]{1,0:T(8,128)(2,1)}, bf16[256,3072]{1,0:T(8,128)(2,1)S(1)}, u32[]{:S(2)}) %copy-start.1) | copy-done | bytes 1572888
  72.0 2.1 %collective-permute-done.6 = bf16[4,32,3072]{2,1,0:T(8,128)(2,1)} collective-permute-done((bf16[4,32,3072]{2,1,0:T(8,128)(2,1)S(1)}, bf16[4,32,3072]{2,1,0:T(8,128)(2,1)}, u32[]{:S(2)}, u32[]{:S(2)}) %collective-permute-start.6) | collective-permute-done | bytes 786464 | tf_op jit(solution)/shard_map/reduce/ppermute | solution.py:19
  74.1 1.6 %fusion = bf16[4,32,3072]{2,1,0:T(8,128)(2,1)S(1)} fusion(bf16[4,32,3072]{2,1,0:T(8,128)(2,1)} %collective-permute-done.6, bf16[4,2,32,3072]{3,2,1,0:T(8,128)(2,1)} %bitcast.120, s32[]{:T(128)S(6)} %select_n.129), kind=kLoop, calls=%fused_computation.2 | loop fusion | flops 1572864 | bytes 2359300 | tf_op jit(solution)/shard_map/reduce/convert_element_type | solution.py:191
  76.4 5.8 %collective-permute-start.9 = (bf16[2,16,3072]{2,1,0:T(8,128)(2,1)}, bf16[2,16,3072]{2,1,0:T(8,128)(2,1)}, u32[]{:S(2)}, u32[]{:S(2)}) collective-permute-start(bf16[2,16,3072]{2,1,0:T(8,128)(2,1)} %pad_maximum_fusion.1), channel_id=1, source_target_pairs={{0,6},{1,7},{2,0},{3,1},{4,2},{5,3},{6,4},{7,5},{8,14},{9,15},{10,... | collective-permute-start | bytes 589832 | tf_op jit(solution)/shard_map/reduce/ppermute | solution.py:19
  82.9 8.4 %collective-permute-done.9 = bf16[2,16,3072]{2,1,0:T(8,128)(2,1)} collective-permute-done((bf16[2,16,3072]{2,1,0:T(8,128)(2,1)}, bf16[2,16,3072]{2,1,0:T(8,128)(2,1)}, u32[]{:S(2)}, u32[]{:S(2)}) %collective-permute-start.9) | collective-permute-done | bytes 196640 | tf_op jit(solution)/shard_map/reduce/ppermute | solution.py:19
  91.4 5.0 %collective-permute-done.7 = bf16[2,16,3072]{2,1,0:T(8,128)(2,1)} collective-permute-done((bf16[2,16,3072]{2,1,0:T(8,128)(2,1)}, bf16[2,16,3072]{2,1,0:T(8,128)(2,1)}, u32[]{:S(2)}, u32[]{:S(2)}) %collective-permute-start.7) | collective-permute-done | bytes 196640 | tf_op jit(solution)/shard_map/reduce/ppermute | solution.py:19
  96.4 1.0 fusion.34
  97.4 4.1 %collective-permute-start.10 = (bf16[16,3072]{1,0:T(8,128)(2,1)S(1)}, bf16[16,3072]{1,0:T(8,128)(2,1)S(1)}, u32[]{:S(2)}, u32[]{:S(2)}) collective-permute-start(bf16[16,3072]{1,0:T(8,128)(2,1)S(1)} %get-tuple-element.24), channel_id=1, source_target_pairs={{0,6},{1,7},{2,0},{3,1},{4,2},{5,3},{6,4},{7,5},{8,14},{9,15},{10,... | collective-permute-start | bytes 294920 | tf_op jit(solution)/shard_map/reduce/ppermute | solution.py:19
  101.6 1.9 %fusion.1 = f32[1,3,128,256]{3,2,1,0:T(8,128)} fusion(bf16[3,128,256]{2,1,0:T(8,128)(2,1)S(1)} %reshape.142, bf16[256,3,128]{0,2,1:T(8,128)(2,1)S(1)} %bitcast.125, f32[256,3]{0,1:T(4,128)S(1)} %get-tuple-element.39, f32[3]{0:T(128)S(1)} %exp.51, bf16[256,512]{1,0:T(8,128)(2,1)} %param.19), kind=kOutput, calls=%fused_computation.4 | convolution fusion | flops 50921472 | bytes 920588 | tf_op jit(solution)/shard_map/mamba/shp,sn->hpn/dot_general | solution.py:153
  103.4 1.9 %collective-permute-done.8 = bf16[16,3072]{1,0:T(8,128)(2,1)S(1)} collective-permute-done((bf16[16,3072]{1,0:T(8,128)(2,1)S(1)}, bf16[16,3072]{1,0:T(8,128)(2,1)S(1)}, u32[]{:S(2)}, u32[]{:S(2)}) %collective-permute-start.8) | collective-permute-done | bytes 98336 | tf_op jit(solution)/shard_map/reduce/ppermute | solution.py:19
  105.3 1.0 fusion.22
  (71 shorter events, 8.8 us)
Async XLA Ops:
  0.6 64.4 %copy-start = (bf16[384,3072]{1,0:T(8,128)(2,1)S(1)}, bf16[384,3072]{1,0:T(8,128)(2,1)}, u32[]{:S(2)}) copy-start(bf16[384,3072]{1,0:T(8,128)(2,1)} %param.26) | copy-start | bytes 7077892
  3.6 13.4 %copy-start.6 = (s32[4]{0:T(128)S(1)}, s32[4]{0:T(128)}, u32[]{:S(2)}) copy-start(s32[4]{0:T(128)} %param.29) | copy-start | bytes 52
  3.6 22.4 %copy-start.10 = (f32[3]{0:T(128)S(1)}, f32[3]{0:T(128)}, u32[]{:S(2)}) copy-start(f32[3]{0:T(128)} %param.21) | copy-start | bytes 40
  4.8 21.8 %all-to-all-start = ((bf16[32,48,256]{2,1,0:T(8,128)(2,1)}), bf16[32,48,256]{2,1,0:T(8,128)(2,1)S(1)}, u32[]{:S(2)}, u32[]{:S(2)}) async-start(bf16[32,48,256]{2,1,0:T(8,128)(2,1)} %maximum_maximum_fusion), calls=%async_computation | async-start | bytes 1572864 | tf_op jit(solution)/shard_map/spread/all_to_all | solution.py:112
  13.4 22.5 %copy-start.5 = (f32[256,3]{0,1:T(4,128)S(1)}, f32[256,3]{0,1:T(4,128)}, u32[]{:S(2)}) copy-start(f32[256,3]{0,1:T(4,128)} %param.20) | copy-start | bytes 9220
  13.4 42.9 %collective-permute-start.1 = (bf16[256,128]{1,0:T(8,128)(2,1)}, bf16[256,128]{1,0:T(8,128)(2,1)}, u32[]{:S(2)}, u32[]{:S(2)}) collective-permute-start(bf16[256,128]{1,0:T(8,128)(2,1)} %q0.1), channel_id=1, source_target_pairs={{0,2},{1,3},{2,0},{3,1},{4,6},{5,7},{6,4},{7,5},{8,10},{9,11},{10,... | collective-permute-start | bytes 196616 | tf_op jit(solution)/shard_map/queries_exchange/ppermute | solution.py:19
  16.8 39.6 %collective-permute-start = (bf16[256,128]{1,0:T(8,128)(2,1)}, bf16[256,128]{1,0:T(8,128)(2,1)}, u32[]{:S(2)}, u32[]{:S(2)}) collective-permute-start(bf16[256,128]{1,0:T(8,128)(2,1)} %q0.1), channel_id=1, source_target_pairs={{0,1},{1,0},{2,3},{3,2},{4,5},{5,4},{6,7},{7,6},{8,9},{9,8},{10,11... | collective-permute-start | bytes 196616 | tf_op jit(solution)/shard_map/queries_exchange/ppermute | solution.py:19
  16.8 39.6 %collective-permute-start.2 = (bf16[256,128]{1,0:T(8,128)(2,1)}, bf16[256,128]{1,0:T(8,128)(2,1)}, u32[]{:S(2)}, u32[]{:S(2)}) collective-permute-start(bf16[256,128]{1,0:T(8,128)(2,1)} %q0.1), channel_id=1, source_target_pairs={{0,3},{1,2},{2,1},{3,0},{4,7},{5,6},{6,5},{7,4},{8,11},{9,10},{10,... | collective-permute-start | bytes 196616 | tf_op jit(solution)/shard_map/queries_exchange/ppermute | solution.py:19
  27.9 13.5 %copy-start.11 = (f32[3]{0:T(128)S(1)}, f32[3]{0:T(128)}, u32[]{:S(2)}) copy-start(f32[3]{0:T(128)} %param.22) | copy-start | bytes 40
  27.9 21.9 %all-to-all-start.1 = ((bf16[32,48,256]{2,1,0:T(8,128)(2,1)}), bf16[32,48,256]{2,1,0:T(8,128)(2,1)S(1)}, u32[]{:S(2)}, u32[]{:S(2)}) async-start(bf16[32,48,256]{2,1,0:T(8,128)(2,1)} %select_select_fusion), calls=%async_computation.1 | async-start | bytes 1572864 | tf_op jit(solution)/shard_map/fetch/all_to_all | solution.py:116
  38.5 11.3 %copy-start.7 = (f32[3]{0:T(128)}, f32[3]{0:T(128)S(1)}, u32[]{:S(2)}) copy-start(f32[3]{0:T(128)S(1)} %slice_reduce_fusion) | copy-start | bytes 40
  56.3 8.7 %copy-start.2 = (f32[256,384]{1,0:T(8,128)S(1)}, f32[256,384]{1,0:T(8,128)}, u32[]{:S(2)}) copy-start(f32[256,384]{1,0:T(8,128)} %copy.31) | copy-start | bytes 1179652
  62.2 5.7 %collective-permute-start.5 = (bf16[144,256]{1,0:T(8,128)(2,1)S(1)}, bf16[144,256]{1,0:T(8,128)(2,1)S(1)}, u32[]{:S(2)}, u32[]{:S(2)}) collective-permute-start(bf16[144,256]{1,0:T(8,128)(2,1)S(1)} %get-tuple-element.36), channel_id=1, source_target_pairs={{0,3},{1,2},{2,1},{3,0},{4,7},{5,6},{6,5},{7,4},{8,11},{9,10},{10,... | collective-permute-start | bytes 221192 | tf_op jit(solution)/shard_map/attention/ppermute | solution.py:19
  62.3 7.3 %collective-permute-start.4 = (bf16[144,256]{1,0:T(8,128)(2,1)S(1)}, bf16[144,256]{1,0:T(8,128)(2,1)S(1)}, u32[]{:S(2)}, u32[]{:S(2)}) collective-permute-start(bf16[144,256]{1,0:T(8,128)(2,1)S(1)} %get-tuple-element.37), channel_id=1, source_target_pairs={{0,2},{1,3},{2,0},{3,1},{4,6},{5,7},{6,4},{7,5},{8,10},{9,11},{10,... | collective-permute-start | bytes 221192 | tf_op jit(solution)/shard_map/attention/ppermute | solution.py:19
  64.7 5.0 %copy-start.9 = (f32[1,256]{1,0:T(1,128)S(1)}, f32[1,256]{1,0:T(1,128)}, u32[]{:S(2)}) copy-start(f32[1,256]{1,0:T(1,128)} %get-tuple-element.10) | copy-start | bytes 3076
  64.7 5.1 %copy-start.3 = (bf16[128,3072]{1,0:T(8,128)(2,1)S(1)}, bf16[128,3072]{1,0:T(8,128)(2,1)}, u32[]{:S(2)}) copy-start(bf16[128,3072]{1,0:T(8,128)(2,1)} %param.25) | copy-start | bytes 2359300
  64.7 5.1 %copy-start.4 = (f32[128,256]{1,0:T(8,128)S(1)}, f32[128,256]{1,0:T(8,128)}, u32[]{:S(2)}) copy-start(f32[128,256]{1,0:T(8,128)} %get-tuple-element.9) | copy-start | bytes 393220
  64.7 5.0 %collective-permute-start.3 = (bf16[144,256]{1,0:T(8,128)(2,1)S(1)}, bf16[144,256]{1,0:T(8,128)(2,1)S(1)}, u32[]{:S(2)}, u32[]{:S(2)}) collective-permute-start(bf16[144,256]{1,0:T(8,128)(2,1)S(1)} %get-tuple-element.38), channel_id=1, source_target_pairs={{0,1},{1,0},{2,3},{3,2},{4,5},{5,4},{6,7},{7,6},{8,9},{9,8},{10,11... | collective-permute-start | bytes 221192 | tf_op jit(solution)/shard_map/attention/ppermute | solution.py:19
  70.4 1.2 %copy-start.1 = (bf16[256,3072]{1,0:T(8,128)(2,1)}, bf16[256,3072]{1,0:T(8,128)(2,1)S(1)}, u32[]{:S(2)}) copy-start(bf16[256,3072]{1,0:T(8,128)(2,1)S(1)} %add_convert_fusion) | copy-start | bytes 4718596
  71.6 2.5 %collective-permute-start.6 = (bf16[4,32,3072]{2,1,0:T(8,128)(2,1)S(1)}, bf16[4,32,3072]{2,1,0:T(8,128)(2,1)}, u32[]{:S(2)}, u32[]{:S(2)}) collective-permute-start(bf16[4,32,3072]{2,1,0:T(8,128)(2,1)S(1)} %dynamic-slice_bitcast_fusion), channel_id=1, source_target_pairs={{0,1},{1,0},{2,3},{3,2},{4,5},{5,4},{6,7},{7,6},{8,9},{9,8},{10,11... | collective-permute-start | bytes 2359304 | tf_op jit(solution)/shard_map/reduce/ppermute | solution.py:19
  72.0 11.0 %copy-start.8 = (f32[3]{0:T(128)S(1)}, f32[3]{0:T(128)}, u32[]{:S(2)}) copy-start(f32[3]{0:T(128)} %copy-done.7) | copy-start | bytes 40
  76.4 15.0 %collective-permute-start.9 = (bf16[2,16,3072]{2,1,0:T(8,128)(2,1)}, bf16[2,16,3072]{2,1,0:T(8,128)(2,1)}, u32[]{:S(2)}, u32[]{:S(2)}) collective-permute-start(bf16[2,16,3072]{2,1,0:T(8,128)(2,1)} %pad_maximum_fusion.1), channel_id=1, source_target_pairs={{0,6},{1,7},{2,0},{3,1},{4,2},{5,3},{6,4},{7,5},{8,14},{9,15},{10,... | collective-permute-start | bytes 589832 | tf_op jit(solution)/shard_map/reduce/ppermute | solution.py:19
  82.9 13.4 %collective-permute-start.7 = (bf16[2,16,3072]{2,1,0:T(8,128)(2,1)}, bf16[2,16,3072]{2,1,0:T(8,128)(2,1)}, u32[]{:S(2)}, u32[]{:S(2)}) collective-permute-start(bf16[2,16,3072]{2,1,0:T(8,128)(2,1)} %pad_maximum_fusion), channel_id=1, source_target_pairs={{0,2},{1,3},{2,4},{3,5},{4,6},{5,7},{6,0},{7,1},{8,10},{9,11},{10,... | collective-permute-start | bytes 589832 | tf_op jit(solution)/shard_map/reduce/ppermute | solution.py:19
  97.3 7.9 %collective-permute-start.8 = (bf16[16,3072]{1,0:T(8,128)(2,1)S(1)}, bf16[16,3072]{1,0:T(8,128)(2,1)S(1)}, u32[]{:S(2)}, u32[]{:S(2)}) collective-permute-start(bf16[16,3072]{1,0:T(8,128)(2,1)S(1)} %get-tuple-element.23), channel_id=1, source_target_pairs={{0,2},{1,3},{2,4},{3,5},{4,6},{5,7},{6,0},{7,1},{8,10},{9,11},{10,... | collective-permute-start | bytes 294920 | tf_op jit(solution)/shard_map/reduce/ppermute | solution.py:19
  97.4 7.9 %collective-permute-start.10 = (bf16[16,3072]{1,0:T(8,128)(2,1)S(1)}, bf16[16,3072]{1,0:T(8,128)(2,1)S(1)}, u32[]{:S(2)}, u32[]{:S(2)}) collective-permute-start(bf16[16,3072]{1,0:T(8,128)(2,1)S(1)} %get-tuple-element.24), channel_id=1, source_target_pairs={{0,6},{1,7},{2,0},{3,1},{4,2},{5,3},{6,4},{7,5},{8,14},{9,15},{10,... | collective-permute-start | bytes 294920 | tf_op jit(solution)/shard_map/reduce/ppermute | solution.py:19
